TPU v7x, 32 devices: a whole 2x2x4 slice. The times are simulated.
32 devices in a mesh: prompt: 8 (over y, x, core), seq: 4 (over z).
Axes of the slice: x: 2, y: 2, z: 4, core: 2. Of those that a mesh axis runs over, the one named last changes fastest.
Arguments:
- queries: bfloat16 [8, 512, 4096], P('prompt', 'seq'), may hold values from -8 to 8
- self_keys: bfloat16 [8, 512, 4096], P('prompt', 'seq'), may hold values from -8 to 8
- self_values: bfloat16 [8, 512, 4096], P('prompt', 'seq'), may hold values from -6 to 6
- cross_queries: bfloat16 [8, 512, 4096], P('prompt', 'seq')
- context: bfloat16 [8, 512, 5120], P('prompt', 'seq')
- key_weight: bfloat16 [5120, 4096], P('prompt', 'seq')
- value_weight: bfloat16 [5120, 4096], P('prompt', 'seq'), may hold values from -0.078125 to 0.078125
- lengths: int32 [8], P('prompt'), may hold values from 64 to 512, as said below
Outputs:
- attended: bfloat16 [8, 512, 4096], P('prompt', 'seq')
Inputs may be any that keep to these rules, and one draw needn't show every extreme that they name: `lengths`: each prompt's number of text tokens; some prompt has all 512.
All inputs are finite; a program needn't handle non-finite values.
Results may differ from a plain program's by a relative error of at most 0.007.
Values may be sent and summed in bfloat16 or wider, within the bound.
A program may use at most 128 MiB of HBM per device.

v0:
```python
import math
import jax
import jax.numpy as jnp
from jax import lax
from jax.sharding import PartitionSpec as P

HD = 128


def head_attend(query_rows, key_rows, value_rows, length, head_count):
    scaling = 1.0 / math.sqrt(HD)
    row_count = query_rows.shape[0]
    key_count = key_rows.shape[0]
    query_split = query_rows.reshape(row_count, head_count, HD)
    key_split = key_rows.reshape(key_count, head_count, HD)
    value_split = value_rows.reshape(key_count, head_count, HD)
    scores = (
        jnp.einsum("rhd,lhd->hrl", query_split, key_split, preferred_element_type=jnp.float32)
        * scaling
    )
    if length is None:
        row_max = jnp.max(scores, axis=2)
        weights = jnp.exp(scores - row_max[:, :, None])
    else:
        usable = (jnp.arange(key_count, dtype=jnp.int32) < length)[None, None, :]
        row_max = jnp.max(jnp.where(usable, scores, -jnp.inf), axis=2)
        shifted = jnp.where(usable, scores, row_max[:, :, None]) - row_max[:, :, None]
        weights = jnp.where(usable, jnp.exp(shifted), jnp.zeros_like(shifted))
    totals = jnp.sum(weights, axis=2)
    mixed = jnp.einsum(
        "hrl,lhd->rhd",
        weights.astype(jnp.bfloat16),
        value_split,
        preferred_element_type=jnp.float32,
    )
    return (
        (mixed / jnp.transpose(totals)[:, :, None])
        .reshape(row_count, head_count * HD)
        .astype(jnp.bfloat16)
    )


def by_blocks(function, query_rows):
    row_count = query_rows.shape[0]
    block_rows = math.gcd(row_count, 512)
    stacked = query_rows.reshape(row_count // block_rows, block_rows, query_rows.shape[1])
    return lax.map(function, stacked).reshape(row_count, -1)


def self_attend(query_heads, key_heads, value_heads, head_count):

    def self_run_block(block):
        return head_attend(block, key_heads, value_heads, None, head_count)

    return by_blocks(self_run_block, query_heads)


def cross_attend(query_rows, key_rows, value_rows, length, head_count):

    def cross_run_block(block):
        return head_attend(block, key_rows, value_rows, length, head_count)

    return by_blocks(cross_run_block, query_rows)


def body(
    queries, self_keys, self_values, cross_queries, context, key_weight, value_weight, lengths
):
    query_local = queries[0]
    key_local = self_keys[0]
    value_local = self_values[0]
    cross_local = cross_queries[0]
    length = lengths[0]
    head_local = key_weight.shape[1] // HD
    text_full = lax.all_gather(context[0], "seq", axis=0, tiled=True)
    key_sums = jnp.dot(
        text_full,
        lax.all_gather(key_weight, "prompt", axis=0, tiled=True),
        preferred_element_type=jnp.float32,
    )
    value_sums = jnp.dot(
        text_full,
        lax.all_gather(value_weight, "prompt", axis=0, tiled=True),
        preferred_element_type=jnp.float32,
    )
    text_keys = key_sums.astype(jnp.bfloat16)
    text_values = value_sums.astype(jnp.bfloat16)
    query_heads, key_heads, value_heads, cross_heads = (
        lax.all_to_all(query_local, "seq", split_axis=1, concat_axis=0, tiled=True),
        lax.all_to_all(key_local, "seq", split_axis=1, concat_axis=0, tiled=True),
        lax.all_to_all(value_local, "seq", split_axis=1, concat_axis=0, tiled=True),
        lax.all_to_all(cross_local, "seq", split_axis=1, concat_axis=0, tiled=True),
    )
    self_heads = self_attend(query_heads, key_heads, value_heads, head_local)
    cross_part = cross_attend(cross_heads, text_keys, text_values, length, head_local)
    summed = (self_heads.astype(jnp.float32) + cross_part.astype(jnp.float32)).astype(jnp.bfloat16)
    attended = lax.all_to_all(summed, "seq", split_axis=0, concat_axis=1, tiled=True)
    return attended[None]


def solution(mesh):
    in_specs = (
        P("prompt", "seq", None),
        P("prompt", "seq", None),
        P("prompt", "seq", None),
        P("prompt", "seq", None),
        P("prompt", "seq", None),
        P("prompt", "seq"),
        P("prompt", "seq"),
        P("prompt"),
    )
    out_specs = P("prompt", "seq", None)
    return jax.shard_map(body, mesh=mesh, in_specs=in_specs, out_specs=out_specs, check_vma=False)
```

profile of v0, /device:TPU:0, one launch (start us, length us, event | category | flops | bytes accessed | tf_op | source)
XLA Modules:
  0.0 361.7 jit_solution(14141983873178840253)
XLA Ops:
  8.7 1.9 all_to_all.58
  11.9 6.3 %all-to-all-start = ((bf16[128,4,1024]{2,0,1:T(8,128)(2,1)}), bf16[128,4,1024]{2,0,1:T(8,128)(2,1)S(1)}, u32[]{:S(2)}, u32[]{:S(2)}) async-start(bf16[128,4,1024]{2,0,1:T(8,128)(2,1)} %copy.28), calls=%async_computation | async-start | bytes 2097152 | tf_op jit(solution)/shard_map/all_to_all | solution.py:89
  20.3 52.6 %all-to-all-done = bf16[128,4,1024]{2,0,1:T(8,128)(2,1)S(1)} async-done(((bf16[128,4,1024]{2,0,1:T(8,128)(2,1)}), bf16[128,4,1024]{2,0,1:T(8,128)(2,1)S(1)}, u32[]{:S(2)}, u32[]{:S(2)}) %all-to-all-start) | async-done | bytes 1048608 | tf_op jit(solution)/shard_map/all_to_all | solution.py:89
  72.9 3.5 all-to-all-start.1
  76.4 1.9 all_to_all.64
  79.6 46.6 %all-to-all-done.1 = bf16[128,4,1024]{2,0,1:T(8,128)(2,1)S(1)} async-done(((bf16[128,4,1024]{2,0,1:T(8,128)(2,1)}), bf16[128,4,1024]{2,0,1:T(8,128)(2,1)S(1)}, u32[]{:S(2)}, u32[]{:S(2)}) %all-to-all-start.1) | async-done | bytes 1048608 | tf_op jit(solution)/shard_map/all_to_all | solution.py:90
  126.2 7.5 %all-to-all-start.2 = ((bf16[128,4,1024]{2,0,1:T(8,128)(2,1)}), bf16[128,4,1024]{2,0,1:T(8,128)(2,1)S(1)}, u32[]{:S(2)}, u32[]{:S(2)}) async-start(bf16[128,4,1024]{2,0,1:T(8,128)(2,1)} %copy.32), calls=%async_computation.2 | async-start | bytes 2097152 | tf_op jit(solution)/shard_map/all_to_all | solution.py:91
  133.7 2.6 all_to_all.67
  136.3 2.5 copy.35
  138.9 32.6 %all-to-all-done.2 = bf16[128,4,1024]{2,0,1:T(8,128)(2,1)S(1)} async-done(((bf16[128,4,1024]{2,0,1:T(8,128)(2,1)}), bf16[128,4,1024]{2,0,1:T(8,128)(2,1)S(1)}, u32[]{:S(2)}, u32[]{:S(2)}) %all-to-all-start.2) | async-done | bytes 1048608 | tf_op jit(solution)/shard_map/all_to_all | solution.py:91
  171.5 4.4 %all-to-all-start.3 = ((bf16[128,4,1024]{2,0,1:T(8,128)(2,1)}), bf16[128,4,1024]{2,0,1:T(8,128)(2,1)}, u32[]{:S(2)}, u32[]{:S(2)}) async-start(bf16[128,4,1024]{2,0,1:T(8,128)(2,1)} %copy.35), calls=%async_computation.3 | async-start | bytes 2097152 | tf_op jit(solution)/shard_map/all_to_all | solution.py:92
  177.2 1.5 copy.51
  178.7 20.3 %all-to-all-done.3 = bf16[128,4,1024]{2,0,1:T(8,128)(2,1)} async-done(((bf16[128,4,1024]{2,0,1:T(8,128)(2,1)}), bf16[128,4,1024]{2,0,1:T(8,128)(2,1)}, u32[]{:S(2)}, u32[]{:S(2)}) %all-to-all-start.3) | async-done | bytes 1048608 | tf_op jit(solution)/shard_map/all_to_all | solution.py:92
  199.0 2.5 copy.52
  202.7 3.5 copy-done
  206.3 1.4 fusion
  207.7 30.1 %all-gather.5.cloned.1.call-done = bf16[5120,1024]{1,0:T(8,128)(2,1)} async-done(((bf16[640,1024]{1,0:T(8,128)(2,1)}), bf16[5120,1024]{1,0:T(8,128)(2,1)}) %all-gather.5.cloned.1.call-update) | async-done | bytes 10485776 | tf_op jit(solution)/shard_map/all_gather | solution.py:83
  237.8 9.8 %fusion.16 = bf16[512,1024]{1,0:T(8,128)(2,1)S(1)} fusion(bf16[5120,1024]{1,0:T(8,128)(2,1)} %all-gather.5.cloned.1.call-done, bf16[1,512,5120]{2,1,0:T(8,128)(2,1)} %all-gather.9.cloned.1.call-done), kind=kOutput, calls=%fused_computation.22 | convolution fusion | flops 5369233408 | bytes 16777216 | tf_op jit(solution)/shard_map/dot_general | solution.py:81
  248.2 54.7 %all-gather.7.cloned.1.call-done = bf16[5120,1024]{1,0:T(8,128)(2,1)} async-done(((bf16[640,1024]{1,0:T(8,128)(2,1)}), bf16[5120,1024]{1,0:T(8,128)(2,1)}) %all-gather.7.cloned.1.call-update) | async-done | bytes 10485776 | tf_op jit(solution)/shard_map/all_gather | solution.py:78
  302.8 9.8 %fusion.22 = bf16[64,8,8,128]{3,2,1,0:T(8,128)(2,1)S(1)} fusion(bf16[5120,1024]{1,0:T(8,128)(2,1)} %all-gather.7.cloned.1.call-done, bf16[1,512,5120]{2,1,0:T(8,128)(2,1)} %all-gather.9.cloned.1.call-done), kind=kOutput, calls=%fused_computation.24 | convolution fusion | flops 5369233408 | bytes 16777216 | tf_op jit(solution)/shard_map/dot_general | solution.py:76
  314.0 2.4 bitcast_reduce_fusion
  316.5 2.5 fusion.12
  319.0 2.5 add_convert_fusion
  322.7 30.5 %all_to_all.77 = bf16[4,128,1024]{2,1,0:T(8,128)(2,1)S(1)} all-to-all(bf16[4,128,1024]{2,1,0:T(8,128)(2,1)S(1)} %convert_element_type.54), channel_id=1, replica_groups=mesh['prompt'=8,'seq'=4] {'seq'}, dimensions={0} | all-to-all | bytes 2097152 | tf_op jit(solution)/shard_map/all_to_all | solution.py:97
  (33 shorter events, 13.7 us)
Async XLA Ops:
  6.5 11.7 %copy-start.2 = (bf16[1,128,4096]{2,1,0:T(8,128)(2,1)S(1)}, bf16[1,128,4096]{2,1,0:T(8,128)(2,1)}, u32[]{:S(2)}) copy-start(bf16[1,128,4096]{2,1,0:T(8,128)(2,1)} %param.9) | copy-start | bytes 3145732
  6.5 201.1 %all-gather.9.cloned.1.call-start = ((), (), s32[]{:S(2)}) async-start(), calls=%async_computation.7 | async-start | bytes 6553600 | tf_op jit(solution)/shard_map/all_gather | solution.py:75
  7.3 230.5 %all-gather.5.cloned.1.call-start = ((), (), s32[]{:S(2)}) async-start(), calls=%async_computation.5 | async-start | bytes 11796480 | tf_op jit(solution)/shard_map/all_gather | solution.py:83
  8.0 294.8 %all-gather.7.cloned.1.call-start = ((), (), s32[]{:S(2)}) async-start(), calls=%async_computation.6 | async-start | bytes 11796480 | tf_op jit(solution)/shard_map/all_gather | solution.py:78
  11.9 61.0 %all-to-all-start = ((bf16[128,4,1024]{2,0,1:T(8,128)(2,1)}), bf16[128,4,1024]{2,0,1:T(8,128)(2,1)S(1)}, u32[]{:S(2)}, u32[]{:S(2)}) async-start(bf16[128,4,1024]{2,0,1:T(8,128)(2,1)} %copy.28), calls=%async_computation | async-start | bytes 2097152 | tf_op jit(solution)/shard_map/all_to_all | solution.py:89
  72.9 53.3 %all-to-all-start.1 = ((bf16[128,4,1024]{2,0,1:T(8,128)(2,1)}), bf16[128,4,1024]{2,0,1:T(8,128)(2,1)S(1)}, u32[]{:S(2)}, u32[]{:S(2)}) async-start(bf16[128,4,1024]{2,0,1:T(8,128)(2,1)} %copy.29), calls=%async_computation.1 | async-start | bytes 2097152 | tf_op jit(solution)/shard_map/all_to_all | solution.py:90
  126.2 45.3 %all-to-all-start.2 = ((bf16[128,4,1024]{2,0,1:T(8,128)(2,1)}), bf16[128,4,1024]{2,0,1:T(8,128)(2,1)S(1)}, u32[]{:S(2)}, u32[]{:S(2)}) async-start(bf16[128,4,1024]{2,0,1:T(8,128)(2,1)} %copy.32), calls=%async_computation.2 | async-start | bytes 2097152 | tf_op jit(solution)/shard_map/all_to_all | solution.py:91
  171.5 5.1 %copy-start.1 = (bf16[128,4,1024]{2,0,1:T(8,128)(2,1)}, bf16[128,4,1024]{2,0,1:T(8,128)(2,1)S(1)}, u32[]{:S(2)}) copy-start(bf16[128,4,1024]{2,0,1:T(8,128)(2,1)S(1)} %all-to-all-done.2) | copy-start | bytes 3145732
  171.5 27.5 %all-to-all-start.3 = ((bf16[128,4,1024]{2,0,1:T(8,128)(2,1)}), bf16[128,4,1024]{2,0,1:T(8,128)(2,1)}, u32[]{:S(2)}, u32[]{:S(2)}) async-start(bf16[128,4,1024]{2,0,1:T(8,128)(2,1)} %copy.35), calls=%async_computation.3 | async-start | bytes 2097152 | tf_op jit(solution)/shard_map/all_to_all | solution.py:92
  202.7 3.5 copy-start
  248.2 64.5 %copy-start.3 = (bf16[64,8,8,128]{3,2,1,0:T(8,128)(2,1)S(1)}, bf16[64,8,8,128]{3,2,1,0:T(8,128)(2,1)}, u32[]{:S(2)}) copy-start(bf16[64,8,8,128]{3,2,1,0:T(8,128)(2,1)} %copy.52) | copy-start | bytes 3145732
  314.0 5.0 %slice-start = ((s8[8388608]{0:T(1024)(128)(4,1)}), s8[4194304]{0:T(1024)(128)(4,1)S(1)}, s32[]{:S(2)}) async-start(s8[8388608]{0:T(1024)(128)(4,1)} %bitcast.60), calls=%async_computation.8 | async-start | bytes 8388608
  316.5 2.5 slice-start.1
Sparse Core Ops, SparseCore 0:
  8.9 164.6 all-gather.8
  175.5 62.2 all-gather.4
  239.7 63.1 all-gather.6
where the time goes:
time: 362 us
  waiting for transfers between devices  239 us (66%)
  blocking collectives  30.5 us (8%)
  matrix products  27.2 us (8%)
  local copies, waits for them, and re-layouts  25.3 us (7%)
  starting transfers between devices  21.9 us (6%)
  between operations  14 us (4%)
  other arithmetic  3.83 us (1%)
    all_gather x1, waiting for transfers between devices, body(): lax.all_gather(key_weight, 'prompt', axis=0, tiled=True)  54.7 us
    all_to_all x1, waiting for transfers between devices, body(): lax.all_to_all(query_local, 'seq', split_axis=1, concat_axis=0, tiled=True)  52.6 us
    all_to_all x1, waiting for transfers between devices, body(): lax.all_to_all(key_local, 'seq', split_axis=1, concat_axis=0, tiled=True)  46.6 us
    all_to_all x1, waiting for transfers between devices, body(): lax.all_to_all(value_local, 'seq', split_axis=1, concat_axis=0, tiled=True)  32.6 us
    all_to_all x1, blocking collectives, body(): lax.all_to_all(summed, 'seq', split_axis=0, concat_axis=1, tiled=True)  30.5 us
    all_gather x1, waiting for transfers between devices, body(): lax.all_gather(value_weight, 'prompt', axis=0, tiled=True)  30.1 us
    all_to_all x1, waiting for transfers between devices, body(): lax.all_to_all(cross_local, 'seq', split_axis=1, concat_axis=0, tiled=True)  20.3 us
    dot_general x1, matrix products, body(): jnp.dot(text_full, lax.all_gather(key_weight, 'prompt', axis=0, tiled=Tru...  9.82 us
  transfers between devices with their start and end apart: 7, of which 6 were waited for; matrix products, arithmetic and copies ran while one was open for 7% of the time, Pallas kernels for 0%

commit v1 on v0

--- a/solution.py
+++ b/solution.py
@@ -5,6 +5,28 @@
 from jax.sharding import PartitionSpec as P
 
 HD = 128
+
+
+def in_order(tiles, dim):
+    tiles = jnp.moveaxis(tiles, 0, dim)
+    dims = tiles.shape
+    return tiles.reshape(*dims[:dim], dims[dim] * dims[dim + 1], *dims[dim + 2 :])
+
+
+def ring_gather(x, axis, dim):
+    size = lax.axis_size(axis)
+    pairs = [(i, (i + 1) % size) for i in range(size)]
+    back = [(b, a) for a, b in pairs]
+    lower, upper = ([], [])
+    for step in range(size - 1):
+        if step % 2 == 0:
+            lower.append(lax.ppermute(lower[-1] if lower else x, axis, pairs))
+        else:
+            upper.append(lax.ppermute(upper[-1] if upper else x, axis, back))
+    blocks = jnp.stack([*lower[::-1], x, *upper])
+    shift = lax.axis_index(axis) - len(lower)
+    blocks = blocks[(jnp.arange(size) - shift) % size]
+    return in_order(blocks, dim)
 
 
 def head_attend(query_rows, key_rows, value_rows, length, head_count):
@@ -79,9 +101,7 @@
         preferred_element_type=jnp.float32,
     )
     value_sums = jnp.dot(
-        text_full,
-        lax.all_gather(value_weight, "prompt", axis=0, tiled=True),
-        preferred_element_type=jnp.float32,
+        text_full, ring_gather(value_weight, "prompt", 0), preferred_element_type=jnp.float32
     )
     text_keys = key_sums.astype(jnp.bfloat16)
     text_values = value_sums.astype(jnp.bfloat16)

time: 362 us -> 346 us (0.956)
  waiting for transfers between devices: 239 us -> 191 us
  local copies, waits for them, and re-layouts: 25.3 us -> 48.2 us
  starting transfers between devices: 21.9 us -> 28.2 us
    ppermute x0 -> x7, waiting for transfers between devices: none -> 72.7 us  [the longest x4 44.3 us: ring_gather(): lower.append(lax.ppermute(lower[-1] if lower else x, axis, pairs))]
    all_gather x1, waiting for transfers between devices: 54.7 us -> 0.01 us  [body(): lax.all_gather(key_weight, 'prompt', axis=0, tiled=True)]
    all_to_all x1, waiting for transfers between devices: 46.6 us -> 2.18 us  [body(): lax.all_to_all(key_local, 'seq', split_axis=1, concat_axis=0, tiled=True)]
    all_to_all x1, waiting for transfers between devices: 20.3 us -> 52.6 us  [body(): lax.all_to_all(cross_local, 'seq', split_axis=1, concat_axis=0, tiled=True)]
    all_gather x1 -> x0, waiting for transfers between devices: 30.1 us -> none  [body(): lax.all_gather(value_weight, 'prompt', axis=0, tiled=True)]
    all_to_all x1, waiting for transfers between devices: 32.6 us -> 15.3 us  [body(): lax.all_to_all(value_local, 'seq', split_axis=1, concat_axis=0, tiled=True)]
    unnamed x16 -> x23, local copies, waits for them, and re-layouts: 8.07 us -> 20.7 us
    gather x0 -> x1, local copies, waits for them, and re-layouts: none -> 9.65 us  [ring_gather(): blocks = blocks[(jnp.arange(size) - shift) % size]]
  transfers between devices with their start and end apart: 7 -> 13, of which waited for: 6 -> 9; matrix products, arithmetic and copies ran while one was open for 7% -> 15% of each run, Pallas kernels for 0% -> 0%
where the time goes in v1:
time: 346 us; the launch traced here: 344 us
  waiting for transfers between devices  191 us (55%)
  local copies, waits for them, and re-layouts  48.2 us (14%)
  blocking collectives  30.8 us (9%)
  starting transfers between devices  28.2 us (8%)
  matrix products  28.2 us (8%)
  between operations  14.3 us (4%)
  other arithmetic  3.86 us (1%)
    all_to_all x1, waiting for transfers between devices, body(): lax.all_to_all(cross_local, 'seq', split_axis=1, concat_axis=0, tiled=True)  52.6 us
    all_to_all x1, waiting for transfers between devices, body(): lax.all_to_all(query_local, 'seq', split_axis=1, concat_axis=0, tiled=True)  46.5 us
    ppermute x4, waiting for transfers between devices, ring_gather(): lower.append(lax.ppermute(lower[-1] if lower else x, axis, pairs))  44.3 us
    all_to_all x1, blocking collectives, body(): lax.all_to_all(summed, 'seq', split_axis=0, concat_axis=1, tiled=True)  30.8 us
    ppermute x3, waiting for transfers between devices, ring_gather(): upper.append(lax.ppermute(upper[-1] if upper else x, axis, back))  28.4 us
    unnamed x23, local copies, waits for them, and re-layouts  20.7 us
    all_to_all x1, waiting for transfers between devices, body(): lax.all_to_all(value_local, 'seq', split_axis=1, concat_axis=0, tiled=True)  15.3 us
    dot_general x1, matrix products, body(): jnp.dot(text_full, ring_gather(value_weight, 'prompt', 0), preferred_elem...  10.7 us
  transfers between devices with their start and end apart: 13, of which 9 were waited for; matrix products, arithmetic and copies ran while one was open for 15% of the time, Pallas kernels for 0%

profile of v1, /device:TPU:0, one launch (start us, length us, event | category | flops | bytes accessed | tf_op | source)
XLA Modules:
  0.0 344.3 jit_solution(3895211516102057017)
XLA Ops:
  11.1 6.3 %all-to-all-start.3 = ((bf16[128,4,1024]{2,0,1:T(8,128)(2,1)}), bf16[128,4,1024]{2,0,1:T(8,128)(2,1)S(1)}, u32[]{:S(2)}, u32[]{:S(2)}) async-start(bf16[128,4,1024]{2,0,1:T(8,128)(2,1)} %copy.33), calls=%async_computation.3 | async-start | bytes 2097152 | tf_op jit(solution)/shard_map/all_to_all | solution.py:112
  19.6 52.6 %all-to-all-done.3 = bf16[128,4,1024]{2,0,1:T(8,128)(2,1)S(1)} async-done(((bf16[128,4,1024]{2,0,1:T(8,128)(2,1)}), bf16[128,4,1024]{2,0,1:T(8,128)(2,1)S(1)}, u32[]{:S(2)}, u32[]{:S(2)}) %all-to-all-start.3) | async-done | bytes 1048608 | tf_op jit(solution)/shard_map/all_to_all | solution.py:112
  72.2 3.5 %all-to-all-start = ((bf16[128,4,1024]{2,0,1:T(8,128)(2,1)}), bf16[128,4,1024]{2,0,1:T(8,128)(2,1)S(1)}, u32[]{:S(2)}, u32[]{:S(2)}) async-start(bf16[128,4,1024]{2,0,1:T(8,128)(2,1)} %copy.26), calls=%async_computation | async-start | bytes 2097152 | tf_op jit(solution)/shard_map/all_to_all | solution.py:109
  78.9 46.5 %all-to-all-done = bf16[128,4,1024]{2,0,1:T(8,128)(2,1)S(1)} async-done(((bf16[128,4,1024]{2,0,1:T(8,128)(2,1)}), bf16[128,4,1024]{2,0,1:T(8,128)(2,1)S(1)}, u32[]{:S(2)}, u32[]{:S(2)}) %all-to-all-start) | async-done | bytes 1048608 | tf_op jit(solution)/shard_map/all_to_all | solution.py:109
  125.5 7.5 %all-to-all-start.1 = ((bf16[128,4,1024]{2,0,1:T(8,128)(2,1)}), bf16[128,4,1024]{2,0,1:T(8,128)(2,1)S(1)}, u32[]{:S(2)}, u32[]{:S(2)}) async-start(bf16[128,4,1024]{2,0,1:T(8,128)(2,1)} %copy.27), calls=%async_computation.1 | async-start | bytes 2097152 | tf_op jit(solution)/shard_map/all_to_all | solution.py:110
  133.0 2.6 collective-permute-start.4
  135.6 27.8 %collective-permute-done.1 = bf16[640,1024]{1,0:T(8,128)(2,1)} collective-permute-done((bf16[640,1024]{1,0:T(8,128)(2,1)}, bf16[640,1024]{1,0:T(8,128)(2,1)}, u32[]{:S(2)}, u32[]{:S(2)}) %collective-permute-start.1) | collective-permute-done | bytes 1310752 | tf_op jit(solution)/shard_map/ppermute | solution.py:23
  163.4 2.6 all_to_all.64
  166.1 2.5 copy.30
  170.7 4.2 %all-to-all-start.2 = ((bf16[128,4,1024]{2,0,1:T(8,128)(2,1)}), bf16[128,4,1024]{2,0,1:T(8,128)(2,1)}, u32[]{:S(2)}, u32[]{:S(2)}) async-start(bf16[128,4,1024]{2,0,1:T(8,128)(2,1)} %copy.30), calls=%async_computation.2 | async-start | bytes 2097152 | tf_op jit(solution)/shard_map/all_to_all | solution.py:111
  176.7 6.6 %collective-permute-done.2 = bf16[640,1024]{1,0:T(8,128)(2,1)} collective-permute-done((bf16[640,1024]{1,0:T(8,128)(2,1)}, bf16[640,1024]{1,0:T(8,128)(2,1)}, u32[]{:S(2)}, u32[]{:S(2)}) %collective-permute-start.2) | collective-permute-done | bytes 1310752 | tf_op jit(solution)/shard_map/ppermute | solution.py:23
  185.2 15.3 %all-to-all-done.2 = bf16[128,4,1024]{2,0,1:T(8,128)(2,1)} async-done(((bf16[128,4,1024]{2,0,1:T(8,128)(2,1)}), bf16[128,4,1024]{2,0,1:T(8,128)(2,1)}, u32[]{:S(2)}, u32[]{:S(2)}) %all-to-all-start.2) | async-done | bytes 1048608 | tf_op jit(solution)/shard_map/all_to_all | solution.py:111
  204.6 12.7 %collective-permute-done.5 = bf16[640,1024]{1,0:T(8,128)(2,1)} collective-permute-done((bf16[640,1024]{1,0:T(8,128)(2,1)}, bf16[640,1024]{1,0:T(8,128)(2,1)}, u32[]{:S(2)}, u32[]{:S(2)}) %collective-permute-start.5) | collective-permute-done | bytes 1310752 | tf_op jit(solution)/shard_map/ppermute | solution.py:25
  217.4 2.8 collective-permute-start.6
  220.2 9.9 %collective-permute-done.3 = bf16[640,1024]{1,0:T(8,128)(2,1)} collective-permute-done((bf16[640,1024]{1,0:T(8,128)(2,1)}, bf16[640,1024]{1,0:T(8,128)(2,1)}, u32[]{:S(2)}, u32[]{:S(2)}) %collective-permute-start.3) | collective-permute-done | bytes 1310752 | tf_op jit(solution)/shard_map/ppermute | solution.py:23
  232.6 2.5 bitcast_dynamic-update-slice_fusion.6
  240.1 2.5 bitcast_dynamic-update-slice_fusion.3
  245.1 2.5 bitcast_dynamic-update-slice_fusion.1
  247.6 15.7 %collective-permute-done.6 = bf16[640,1024]{1,0:T(8,128)(2,1)S(1)} collective-permute-done((bf16[640,1024]{1,0:T(8,128)(2,1)}, bf16[640,1024]{1,0:T(8,128)(2,1)S(1)}, u32[]{:S(2)}, u32[]{:S(2)}) %collective-permute-start.6) | collective-permute-done | bytes 1310752 | tf_op jit(solution)/shard_map/ppermute | solution.py:25
  264.4 9.7 %gather_fusion = bf16[8,640,1024]{2,1,0:T(8,128)(2,1)} fusion(bf16[8,640,1024]{2,1,0:T(8,128)(2,1)} %bitcast_dynamic-update-slice_fusion, s32[1024]{0:T(1024)S(1)} %pad_clamp_fusion), kind=kCustom, calls=%fused_computation | custom fusion | bytes 20971552 | tf_op jit(solution)/shard_map/gather | solution.py:28
  274.1 10.7 %fusion.19 = bf16[1024,512]{1,0:T(8,128)(2,1)} fusion(bf16[5120,1024]{1,0:T(8,128)(2,1)} %bitcast.83, bf16[1,512,5120]{2,1,0:T(8,128)(2,1)} %all-gather.6.cloned.1.call-done), kind=kOutput, calls=%fused_computation.24 | convolution fusion | flops 5369233408 | bytes 16777216 | tf_op jit(solution)/shard_map/dot_general | solution.py:103
  284.8 9.9 %fusion.22 = bf16[64,8,8,128]{3,2,1,0:T(8,128)(2,1)S(1)} fusion(bf16[5120,1024]{1,0:T(8,128)(2,1)} %all-gather.4.cloned.1.call-done, bf16[1,512,5120]{2,1,0:T(8,128)(2,1)} %all-gather.6.cloned.1.call-done), kind=kOutput, calls=%fused_computation.25 | convolution fusion | flops 5369233408 | bytes 16777216 | tf_op jit(solution)/shard_map/dot_general | solution.py:98
  298.6 2.5 fusion.12
  304.7 30.8 %all_to_all.77 = bf16[4,128,1024]{2,1,0:T(8,128)(2,1)S(1)} all-to-all(bf16[4,128,1024]{2,1,0:T(8,128)(2,1)S(1)} %convert_element_type.58), channel_id=1, replica_groups=mesh['prompt'=8,'seq'=4] {'seq'}, dimensions={0} | all-to-all | bytes 2097152 | tf_op jit(solution)/shard_map/all_to_all | solution.py:117
  (54 shorter events, 39.5 us)
Async XLA Ops:
  6.5 11.0 %copy-start.1 = (bf16[1,128,4096]{2,1,0:T(8,128)(2,1)S(1)}, bf16[1,128,4096]{2,1,0:T(8,128)(2,1)}, u32[]{:S(2)}) copy-start(bf16[1,128,4096]{2,1,0:T(8,128)(2,1)} %param.8) | copy-start | bytes 3145732
  6.5 267.5 %all-gather.6.cloned.1.call-start = ((), (), s32[]{:S(2)}) async-start(), calls=%async_computation.6 | async-start | bytes 6553600 | tf_op jit(solution)/shard_map/all_gather | solution.py:97
  7.3 277.5 %all-gather.4.cloned.1.call-start = ((), (), s32[]{:S(2)}) async-start(), calls=%async_computation.5 | async-start | bytes 11796480 | tf_op jit(solution)/shard_map/all_gather | solution.py:100
  11.1 61.0 %all-to-all-start.3 = ((bf16[128,4,1024]{2,0,1:T(8,128)(2,1)}), bf16[128,4,1024]{2,0,1:T(8,128)(2,1)S(1)}, u32[]{:S(2)}, u32[]{:S(2)}) async-start(bf16[128,4,1024]{2,0,1:T(8,128)(2,1)} %copy.33), calls=%async_computation.3 | async-start | bytes 2097152 | tf_op jit(solution)/shard_map/all_to_all | solution.py:112
  72.2 53.3 %all-to-all-start = ((bf16[128,4,1024]{2,0,1:T(8,128)(2,1)}), bf16[128,4,1024]{2,0,1:T(8,128)(2,1)S(1)}, u32[]{:S(2)}, u32[]{:S(2)}) async-start(bf16[128,4,1024]{2,0,1:T(8,128)(2,1)} %copy.26), calls=%async_computation | async-start | bytes 2097152 | tf_op jit(solution)/shard_map/all_to_all | solution.py:109
  75.7 57.3 %collective-permute-start = (bf16[640,1024]{1,0:T(8,128)(2,1)}, bf16[640,1024]{1,0:T(8,128)(2,1)}, u32[]{:S(2)}, u32[]{:S(2)}) collective-permute-start(bf16[640,1024]{1,0:T(8,128)(2,1)} %param.14), channel_id=1, source_target_pairs={{0,4},{4,8},{8,12},{12,16},{16,20},{20,24},{24,28},{28,0},{1,5},{5... | collective-permute-start | bytes 3932168 | tf_op jit(solution)/shard_map/ppermute | solution.py:23
  125.5 45.3 %all-to-all-start.1 = ((bf16[128,4,1024]{2,0,1:T(8,128)(2,1)}), bf16[128,4,1024]{2,0,1:T(8,128)(2,1)S(1)}, u32[]{:S(2)}, u32[]{:S(2)}) async-start(bf16[128,4,1024]{2,0,1:T(8,128)(2,1)} %copy.27), calls=%async_computation.1 | async-start | bytes 2097152 | tf_op jit(solution)/shard_map/all_to_all | solution.py:110
  133.0 30.4 %collective-permute-start.1 = (bf16[640,1024]{1,0:T(8,128)(2,1)}, bf16[640,1024]{1,0:T(8,128)(2,1)}, u32[]{:S(2)}, u32[]{:S(2)}) collective-permute-start(bf16[640,1024]{1,0:T(8,128)(2,1)} %collective-permute-done), channel_id=1, source_target_pairs={{0,4},{4,8},{8,12},{12,16},{16,20},{20,24},{24,28},{28,0},{1,5},{5... | collective-permute-start | bytes 3932168 | tf_op jit(solution)/shard_map/ppermute | solution.py:23
  133.0 42.7 %collective-permute-start.4 = (bf16[640,1024]{1,0:T(8,128)(2,1)}, bf16[640,1024]{1,0:T(8,128)(2,1)}, u32[]{:S(2)}, u32[]{:S(2)}) collective-permute-start(bf16[640,1024]{1,0:T(8,128)(2,1)} %param.14), channel_id=1, source_target_pairs={{4,0},{8,4},{12,8},{16,12},{20,16},{24,20},{28,24},{0,28},{5,1},{9... | collective-permute-start | bytes 3932168 | tf_op jit(solution)/shard_map/ppermute | solution.py:25
  163.4 19.9 %collective-permute-start.2 = (bf16[640,1024]{1,0:T(8,128)(2,1)}, bf16[640,1024]{1,0:T(8,128)(2,1)}, u32[]{:S(2)}, u32[]{:S(2)}) collective-permute-start(bf16[640,1024]{1,0:T(8,128)(2,1)} %collective-permute-done.1), channel_id=1, source_target_pairs={{0,4},{4,8},{8,12},{12,16},{16,20},{20,24},{24,28},{28,0},{1,5},{5... | collective-permute-start | bytes 3932168 | tf_op jit(solution)/shard_map/ppermute | solution.py:23
  170.7 29.7 %all-to-all-start.2 = ((bf16[128,4,1024]{2,0,1:T(8,128)(2,1)}), bf16[128,4,1024]{2,0,1:T(8,128)(2,1)}, u32[]{:S(2)}, u32[]{:S(2)}) async-start(bf16[128,4,1024]{2,0,1:T(8,128)(2,1)} %copy.30), calls=%async_computation.2 | async-start | bytes 2097152 | tf_op jit(solution)/shard_map/all_to_all | solution.py:111
  175.7 41.7 %collective-permute-start.5 = (bf16[640,1024]{1,0:T(8,128)(2,1)}, bf16[640,1024]{1,0:T(8,128)(2,1)}, u32[]{:S(2)}, u32[]{:S(2)}) collective-permute-start(bf16[640,1024]{1,0:T(8,128)(2,1)} %collective-permute-done.4), channel_id=1, source_target_pairs={{4,0},{8,4},{12,8},{16,12},{20,16},{24,20},{28,24},{0,28},{5,1},{9... | collective-permute-start | bytes 3932168 | tf_op jit(solution)/shard_map/ppermute | solution.py:25
  183.3 46.8 %collective-permute-start.3 = (bf16[640,1024]{1,0:T(8,128)(2,1)}, bf16[640,1024]{1,0:T(8,128)(2,1)}, u32[]{:S(2)}, u32[]{:S(2)}) collective-permute-start(bf16[640,1024]{1,0:T(8,128)(2,1)} %collective-permute-done.2), channel_id=1, source_target_pairs={{0,4},{4,8},{8,12},{12,16},{16,20},{20,24},{24,28},{28,0},{1,5},{5... | collective-permute-start | bytes 3932168 | tf_op jit(solution)/shard_map/ppermute | solution.py:23
  203.2 36.8 %copy-start = (f32[8,512,512]{1,2,0:T(8,128)}, f32[8,512,512]{1,2,0:T(8,128)S(1)}, u32[]{:S(2)}) copy-start(f32[8,512,512]{1,2,0:T(8,128)S(1)} %get-tuple-element.33) | copy-start | bytes 25165828
  217.4 45.9 %collective-permute-start.6 = (bf16[640,1024]{1,0:T(8,128)(2,1)}, bf16[640,1024]{1,0:T(8,128)(2,1)S(1)}, u32[]{:S(2)}, u32[]{:S(2)}) collective-permute-start(bf16[640,1024]{1,0:T(8,128)(2,1)} %collective-permute-done.5), channel_id=1, source_target_pairs={{4,0},{8,4},{12,8},{16,12},{20,16},{24,20},{28,24},{0,28},{5,1},{9... | collective-permute-start | bytes 3932168 | tf_op jit(solution)/shard_map/ppermute | solution.py:25
  284.8 9.9 %copy-start.2 = (bf16[64,8,8,128]{3,2,1,0:T(8,128)(2,1)S(1)}, bf16[64,8,8,128]{3,2,1,0:T(8,128)(2,1)}, u32[]{:S(2)}) copy-start(bf16[64,8,8,128]{3,2,1,0:T(8,128)(2,1)} %copy.48) | copy-start | bytes 3145732
  294.7 3.8 %copy-start.3 = (bf16[1024,512]{1,0:T(8,128)(2,1)S(1)}, bf16[1024,512]{1,0:T(8,128)(2,1)}, u32[]{:S(2)}) copy-start(bf16[1024,512]{1,0:T(8,128)(2,1)} %fusion.19) | copy-start | bytes 3145732
  296.1 5.0 %slice-start = ((s8[8388608]{0:T(1024)(128)(4,1)}), s8[4194304]{0:T(1024)(128)(4,1)S(1)}, s32[]{:S(2)}) async-start(s8[8388608]{0:T(1024)(128)(4,1)} %bitcast.81), calls=%async_computation.7 | async-start | bytes 8388608
  298.6 2.5 slice-start.1
Sparse Core Ops, SparseCore 0:
  8.9 163.9 all-gather.5
  174.8 92.8 all-gather.3
